TPU v7x, 512 devices: a whole 4x8x8 slice. The times are simulated.
512 devices in a mesh: resp: 32 (over x, y), mp: 16 (over z, core).
Axes of the slice: x: 4, y: 8, z: 8, core: 2. Of those that a mesh axis runs over, the one named last changes fastest.
Arguments:
- queries: bfloat16 [32, 512, 4096], P('resp', None, 'mp'), may hold values from -160 to 160
- keys: bfloat16 [32, 512, 512], P('resp'), may hold values from -8 to 8
- values: bfloat16 [32, 512, 512], P('resp'), may hold values from -6 to 6
- out_weight: bfloat16 [4096, 8192], P(None, 'mp'), may hold values from -1.5 to 1.5
- order_bias: float32 [2, 32], replicated, may hold values from -2 to 2
- partners: int32 [32, 6], P('resp'), may hold values from -1 to 31, as said below
- count: int32 [32], P('resp'), may hold values from 1 to 6, as said below
- order: int32 [32, 6], P('resp'), may hold values 0 or 1
Outputs:
- judged: bfloat16 [32, 512, 8192], P('resp', None, 'mp')
Inputs may be any that keep to these rules, and one draw needn't show every extreme that they name: `partners`: slot s of response r is used iff s < count[r]; unused slots hold -1; a used entry names a response other than r at cyclic distance at most 3; the used entries of a row are distinct. `count`: some response has 6 partners and some other has 1.
All inputs are finite; a program needn't handle non-finite values. No bound on the sum of `order` on one device may be relied on, other than what follows from the above.
Results may differ from a plain program's by a relative error of at most 0.0057.
Values may be sent and summed in bfloat16 or wider, within the bound.
A program may use at most 64 MiB of HBM per device.

v0:
```python
import math
import jax
import jax.numpy as jnp
from jax import lax
from jax.sharding import PartitionSpec as P

HQ = 32
KVH = 4
HD = 128
REACH = 3
SLOTS = 6


def shifted(value, axis, steps):
    count = lax.axis_size(axis)
    pairs = [(source, (source + steps) % count) for source in range(count)]
    return lax.ppermute(value, axis, pairs)


def on_device(queries, keys, values, out_weight, order_bias, partners, count, order):
    seq_len = queries.shape[1]
    heads_dev = queries.shape[2] // HD
    group_size = HQ // KVH
    score_scale = 1.0 / math.sqrt(HD)
    first_head = lax.axis_index("mp") * heads_dev
    kv_head = first_head // group_size
    own_keys = lax.dynamic_slice_in_dim(keys[0], kv_head * HD, HD, 1)
    own_values = lax.dynamic_slice_in_dim(values[0], kv_head * HD, HD, 1)
    packed = jnp.stack([own_keys, own_values])
    slot_ids = jnp.arange(SLOTS, dtype=jnp.int32)
    in_use = slot_ids < count[0]
    resp_total = lax.axis_size("resp")
    resp_self = lax.axis_index("resp")
    near_offsets = list(range(1, REACH + 1)) + [-hop_id for hop_id in range(1, REACH + 1)]
    neighbours = []
    for offset in near_offsets:
        neighbours.append(shifted(packed, "resp", -offset))
    stacked = jnp.stack(neighbours)
    distance = (partners[0] - resp_self) % resp_total
    signed = jnp.where(distance <= REACH, distance, distance - resp_total)
    match = (signed[:, None] == jnp.array(near_offsets, jnp.int32)[None, :]) & in_use[:, None]
    flat = stacked.reshape(len(near_offsets), -1)
    picked = jnp.dot(match.astype(jnp.bfloat16), flat, preferred_element_type=jnp.float32)
    picked = picked.astype(jnp.bfloat16).reshape((SLOTS,) + packed.shape)
    key_rows = jnp.concatenate([own_keys[None], picked[:, 0]], 0)
    value_rows = jnp.concatenate([own_values[None], picked[:, 1]], 0)
    query_rows = queries[0].reshape(seq_len, heads_dev, HD)
    scores = (
        jnp.einsum("ihd,sjd->hisj", query_rows, key_rows, preferred_element_type=jnp.float32)
        * score_scale
    )
    bias_dev = lax.dynamic_slice_in_dim(order_bias, first_head, heads_dev, 1)
    slot_bias = jnp.where(order[0][:, None] == 1, bias_dev[1][None, :], bias_dev[0][None, :])
    bias_all = jnp.concatenate([jnp.zeros((1, heads_dev), jnp.float32), slot_bias], 0).T
    scores = scores + bias_all[:, None, :, None]
    causal = jnp.arange(seq_len)[:, None] >= jnp.arange(seq_len)[None, :]
    partner_seen = jnp.broadcast_to(in_use[None, :, None], (seq_len, SLOTS, seq_len))
    visible = jnp.concatenate([causal[:, None, :], partner_seen], 1)
    scores = jnp.where(visible[None], scores, -jnp.inf)
    highest = jnp.max(scores, axis=(2, 3), keepdims=True)
    expo = jnp.exp(scores - highest)
    weights = (expo / jnp.sum(expo, axis=(2, 3), keepdims=True)).astype(jnp.bfloat16)
    attended = jnp.einsum("hisj,sjd->ihd", weights, value_rows, preferred_element_type=jnp.float32)
    attended = attended.astype(jnp.bfloat16).reshape(seq_len, heads_dev * HD)
    judged = jnp.dot(
        lax.all_gather(attended, "mp", axis=1, tiled=True),
        out_weight,
        preferred_element_type=jnp.float32,
    )
    return judged.astype(jnp.bfloat16)[None]


def solution(mesh):
    in_specs = (
        P("resp", None, "mp"),
        P("resp", None, None),
        P("resp", None, None),
        P(None, "mp"),
        P(),
        P("resp", None),
        P("resp"),
        P("resp", None),
    )
    out_specs = P("resp", None, "mp")
    return jax.shard_map(
        on_device, mesh=mesh, in_specs=in_specs, out_specs=out_specs, check_vma=False
    )
```

profile of v0, /device:TPU:1, one launch (start us, length us, event | category | flops | bytes accessed | tf_op | source)
XLA Modules:
  0.0 158.9 jit_solution(16830722555122858521)
XLA Ops:
  6.5 0.0 copy-start
  6.5 0.0 copy-start.4
  6.5 0.0 all-gather.2.cloned.1.call-start
  6.5 1.0 constant_dynamic-slice_fusion.1
  7.6 6.1 %collective-permute-start.5 = (bf16[2,512,128]{2,1,0:T(8,128)(2,1)S(1)}, bf16[2,512,128]{2,1,0:T(8,128)(2,1)S(1)}, u32[]{:S(2)}, u32[]{:S(2)}) collective-permute-start(bf16[2,512,128]{2,1,0:T(8,128)(2,1)S(1)} %pad_maximum_fusion), channel_id=1, source_target_pairs={{0,48},{16,64},{32,80},{48,96},{64,112},{80,128},{96,144},{112,160... | collective-permute-start | bytes 786440 | tf_op jit(solution)/shard_map/ppermute | solution.py:17
  13.7 4.5 %collective-permute-start.4 = (bf16[2,512,128]{2,1,0:T(8,128)(2,1)S(1)}, bf16[2,512,128]{2,1,0:T(8,128)(2,1)S(1)}, u32[]{:S(2)}, u32[]{:S(2)}) collective-permute-start(bf16[2,512,128]{2,1,0:T(8,128)(2,1)S(1)} %pad_maximum_fusion), channel_id=1, source_target_pairs={{0,32},{16,48},{32,64},{48,80},{64,96},{80,112},{96,128},{112,144}... | collective-permute-start | bytes 786440 | tf_op jit(solution)/shard_map/ppermute | solution.py:17
  18.2 2.3 %collective-permute-start.3 = (bf16[2,512,128]{2,1,0:T(8,128)(2,1)S(1)}, bf16[2,512,128]{2,1,0:T(8,128)(2,1)S(1)}, u32[]{:S(2)}, u32[]{:S(2)}) collective-permute-start(bf16[2,512,128]{2,1,0:T(8,128)(2,1)S(1)} %pad_maximum_fusion), channel_id=1, source_target_pairs={{0,16},{16,32},{32,48},{48,64},{64,80},{80,96},{96,112},{112,128},... | collective-permute-start | bytes 786440 | tf_op jit(solution)/shard_map/ppermute | solution.py:17
  20.5 5.8 %collective-permute-start.2 = (bf16[2,512,128]{2,1,0:T(8,128)(2,1)S(1)}, bf16[2,512,128]{2,1,0:T(8,128)(2,1)S(1)}, u32[]{:S(2)}, u32[]{:S(2)}) collective-permute-start(bf16[2,512,128]{2,1,0:T(8,128)(2,1)S(1)} %pad_maximum_fusion), channel_id=1, source_target_pairs={{0,464},{16,480},{32,496},{48,0},{64,16},{80,32},{96,48},{112,64},... | collective-permute-start | bytes 786440 | tf_op jit(solution)/shard_map/ppermute | solution.py:17
  26.3 3.2 %collective-permute-start.1 = (bf16[2,512,128]{2,1,0:T(8,128)(2,1)S(1)}, bf16[2,512,128]{2,1,0:T(8,128)(2,1)S(1)}, u32[]{:S(2)}, u32[]{:S(2)}) collective-permute-start(bf16[2,512,128]{2,1,0:T(8,128)(2,1)S(1)} %pad_maximum_fusion), channel_id=1, source_target_pairs={{0,480},{16,496},{32,0},{48,16},{64,32},{80,48},{96,64},{112,80},{... | collective-permute-start | bytes 786440 | tf_op jit(solution)/shard_map/ppermute | solution.py:17
  29.5 0.1 iota_compare_fusion
  30.3 0.0 copy-done
  30.3 0.1 constant_dynamic-slice_fusion
  30.4 0.1 pad.4.clone
  30.4 1.9 %pad_add_fusion = pred[512,7,512]{0,2,1:T(8,128)(4,1)} fusion(pred[512,1,512]{0,2,1:T(8,128)(4,1)S(1)} %iota_compare_fusion, pred[7]{0:T(512)(128)(4,1)S(1)} %pad.4.clone), kind=kLoop, calls=%fused_computation.6 | loop fusion | flops 1835008 | bytes 2097159 | tf_op jit(solution)/shard_map/concatenate | solution.py:58
  32.3 0.7 compare_bitcast_fusion
  33.0 0.1 broadcast_select_fusion
  33.0 0.0 collective-permute-done.5
  33.0 2.6 %collective-permute-start = (bf16[2,512,128]{2,1,0:T(8,128)(2,1)S(1)}, bf16[2,512,128]{2,1,0:T(8,128)(2,1)S(1)}, u32[]{:S(2)}, u32[]{:S(2)}) collective-permute-start(bf16[2,512,128]{2,1,0:T(8,128)(2,1)S(1)} %pad_maximum_fusion), channel_id=1, source_target_pairs={{0,496},{16,0},{32,16},{48,32},{64,48},{80,64},{96,80},{112,96},{1... | collective-permute-start | bytes 786440 | tf_op jit(solution)/shard_map/ppermute | solution.py:17
  35.7 0.8 copy.11
  36.4 1.7 %reshape_squeeze.3 = bf16[512,2,128]{2,1,0:T(2,128)(2,1)} reshape(bf16[1,512,256]{2,1,0:T(8,128)(2,1)} %param.9) | data formatting | bytes 524288 | tf_op jit(solution)/shard_map/reshape;squeeze | solution.py:47
  38.2 0.0 copy-done.4
  38.2 0.1 stack.32
  38.3 5.9 %collective-permute-done.4 = bf16[2,512,128]{2,1,0:T(8,128)(2,1)S(1)} collective-permute-done((bf16[2,512,128]{2,1,0:T(8,128)(2,1)S(1)}, bf16[2,512,128]{2,1,0:T(8,128)(2,1)S(1)}, u32[]{:S(2)}, u32[]{:S(2)}) %collective-permute-start.4) | collective-permute-done | bytes 262176 | tf_op jit(solution)/shard_map/ppermute | solution.py:17
  44.2 0.1 stack.31
  44.3 0.0 copy-start.3
  44.3 7.6 %collective-permute-done.3 = bf16[2,512,128]{2,1,0:T(8,128)(2,1)S(1)} collective-permute-done((bf16[2,512,128]{2,1,0:T(8,128)(2,1)S(1)}, bf16[2,512,128]{2,1,0:T(8,128)(2,1)S(1)}, u32[]{:S(2)}, u32[]{:S(2)}) %collective-permute-start.3) | collective-permute-done | bytes 262176 | tf_op jit(solution)/shard_map/ppermute | solution.py:17
  51.9 0.9 stack.30
  52.8 0.0 collective-permute-done.2
  52.8 0.9 stack.29
  53.7 2.3 %collective-permute-done.1 = bf16[2,512,128]{2,1,0:T(8,128)(2,1)S(1)} collective-permute-done((bf16[2,512,128]{2,1,0:T(8,128)(2,1)S(1)}, bf16[2,512,128]{2,1,0:T(8,128)(2,1)S(1)}, u32[]{:S(2)}, u32[]{:S(2)}) %collective-permute-start.1) | collective-permute-done | bytes 262176 | tf_op jit(solution)/shard_map/ppermute | solution.py:17
  56.0 0.9 stack.28
  56.9 3.4 %collective-permute-done = bf16[2,512,128]{2,1,0:T(8,128)(2,1)S(1)} collective-permute-done((bf16[2,512,128]{2,1,0:T(8,128)(2,1)S(1)}, bf16[2,512,128]{2,1,0:T(8,128)(2,1)S(1)}, u32[]{:S(2)}, u32[]{:S(2)}) %collective-permute-start) | collective-permute-done | bytes 262176 | tf_op jit(solution)/shard_map/ppermute | solution.py:17
  60.3 0.9 stack.27
  61.2 9.1 %stack.33 = bf16[6,131072]{1,0:T(8,128)(2,1)S(1)} concatenate(bf16[1,131072]{1,0:T(2,128)(2,1)} %stack.27, bf16[1,131072]{1,0:T(2,128)(2,1)} %stack.28, bf16[1,131072]{1,0:T(2,128)(2,1)} %stack.29, bf16[1,131072]{1,0:T(2,128)(2,1)} %stack.30, bf16[1,131072]{1,0:T(2,128)(2,1)S(1)} %stack.31, bf16[1,131072]{1,0:T(2,128)(2,1)S(1)} %stack.32), dimensions={0} | concatenate | bytes 3145728 | tf_op jit(solution)/shard_map/stack | solution.py:38
  70.3 0.0 copy-done.3
  70.3 0.8 fusion.3
  71.1 0.0 copy-start.1
  71.1 0.2 copy.21
  71.3 1.0 fusion.23
  72.3 0.3 copy.19
  72.6 0.2 copy-done.1
  72.9 9.6 %fusion.24 = (f32[2,512]{1,0:T(2,128)S(1)}, f32[2,512,7,512]{1,3,0,2:T(8,128)}) fusion(f32[2,7]{0,1:T(8,128)S(1)} %pad_bitcast_fusion, bf16[512,2,128]{2,1,0:T(2,128)(2,1)} %reshape_squeeze.3, bf16[6,512,128]{2,1,0:T(8,128)(2,1)} %get-tuple-element.6, bf16[1,512,128]{2,1,0:T(8,128)(2,1)S(1)} %get-tuple-element.11, pred[512,7,512]{0,2,1:T(8,128)(4,1)S(1)} %copy-done.1), kind=kOutput, calls=%fused_computation.47 | convolution fusion | flops 956038144 | bytes 17698872 | tf_op jit(solution)/shard_map/ihd,sjd->hisj/dot_general | solution.py:49
  82.4 0.0 copy-start.2
  82.4 7.1 %fusion.1 = f32[2,512]{1,0:T(2,128)S(1)} fusion(f32[2,512,7,512]{1,3,0,2:T(8,128)} %get-tuple-element.10, f32[2,512]{1,0:T(2,128)S(1)} %get-tuple-element.9), kind=kLoop, calls=%fused_computation.5 | loop fusion | flops 7339008 | bytes 14688256 | tf_op jit(solution)/shard_map/reduce_sum | solution.py:62
  89.6 0.0 copy-done.2
  89.6 7.4 %fusion.6 = bf16[128,2,512]{2,0,1:T(8,128)(2,1)} fusion(f32[2,512,7,512]{1,3,0,2:T(8,128)} %get-tuple-element.10, f32[2,512]{1,0:T(2,128)S(1)} %fusion.1, f32[2,512]{1,0:T(2,128)S(1)} %get-tuple-element.9, bf16[6,512,128]{1,2,0:T(8,128)(2,1)S(1)} %bitcast.58, bf16[1,512,128]{1,2,0:T(8,128)(2,1)S(1)} %copy-done.2), kind=kOutput, calls=%fused_computation.12 | convolution fusion | flops 952500224 | bytes 15867904 | tf_op jit(solution)/shard_map/hisj,sjd->ihd/dot_general | solution.py:63
  97.0 0.0 all-gather.2.cloned.1.call-update
  97.0 48.4 %all-gather.2.cloned.1.call-done = bf16[512,4096]{0,1:T(8,128)(2,1)} async-done(((bf16[512,256]{0,1:T(8,128)(2,1)}), bf16[512,4096]{0,1:T(8,128)(2,1)}) %all-gather.2.cloned.1.call-update) | async-done | bytes 4194320 | tf_op jit(solution)/shard_map/all_gather | solution.py:66
  145.4 6.6 %fusion.4 = bf16[1,512,512]{2,1,0:T(8,128)(2,1)} fusion(bf16[512,4096]{0,1:T(8,128)(2,1)} %all-gather.2.cloned.1.call-done, bf16[4096,512]{1,0:T(8,128)(2,1)} %param.12), kind=kOutput, calls=%fused_computation.10 | convolution fusion | flops 2147745792 | bytes 8912896 | tf_op jit(solution)/shard_map/dot_general | solution.py:65
  (5 shorter events, 0.1 us)
Async XLA Ops:
  6.5 23.7 %copy-start = (f32[2,32]{1,0:T(2,128)S(1)}, f32[2,32]{1,0:T(2,128)}, u32[]{:S(2)}) copy-start(f32[2,32]{1,0:T(2,128)} %param.13) | copy-start | bytes 772
  6.5 31.6 %copy-start.4 = (s32[1,6]{1,0:T(1,128)S(1)}, s32[1,6]{1,0:T(1,128)}, u32[]{:S(2)}) copy-start(s32[1,6]{1,0:T(1,128)} %param.14) | copy-start | bytes 76
  6.5 138.9 %all-gather.2.cloned.1.call-start = ((), (), s32[]{:S(2)}) async-start(), calls=%async_computation | async-start | bytes 4456448 | tf_op jit(solution)/shard_map/all_gather | solution.py:66
  7.6 25.5 %collective-permute-start.5 = (bf16[2,512,128]{2,1,0:T(8,128)(2,1)S(1)}, bf16[2,512,128]{2,1,0:T(8,128)(2,1)S(1)}, u32[]{:S(2)}, u32[]{:S(2)}) collective-permute-start(bf16[2,512,128]{2,1,0:T(8,128)(2,1)S(1)} %pad_maximum_fusion), channel_id=1, source_target_pairs={{0,48},{16,64},{32,80},{48,96},{64,112},{80,128},{96,144},{112,160... | collective-permute-start | bytes 786440 | tf_op jit(solution)/shard_map/ppermute | solution.py:17
  13.7 30.5 %collective-permute-start.4 = (bf16[2,512,128]{2,1,0:T(8,128)(2,1)S(1)}, bf16[2,512,128]{2,1,0:T(8,128)(2,1)S(1)}, u32[]{:S(2)}, u32[]{:S(2)}) collective-permute-start(bf16[2,512,128]{2,1,0:T(8,128)(2,1)S(1)} %pad_maximum_fusion), channel_id=1, source_target_pairs={{0,32},{16,48},{32,64},{48,80},{64,96},{80,112},{96,128},{112,144}... | collective-permute-start | bytes 786440 | tf_op jit(solution)/shard_map/ppermute | solution.py:17
  18.2 33.7 %collective-permute-start.3 = (bf16[2,512,128]{2,1,0:T(8,128)(2,1)S(1)}, bf16[2,512,128]{2,1,0:T(8,128)(2,1)S(1)}, u32[]{:S(2)}, u32[]{:S(2)}) collective-permute-start(bf16[2,512,128]{2,1,0:T(8,128)(2,1)S(1)} %pad_maximum_fusion), channel_id=1, source_target_pairs={{0,16},{16,32},{32,48},{48,64},{64,80},{80,96},{96,112},{112,128},... | collective-permute-start | bytes 786440 | tf_op jit(solution)/shard_map/ppermute | solution.py:17
  20.5 32.3 %collective-permute-start.2 = (bf16[2,512,128]{2,1,0:T(8,128)(2,1)S(1)}, bf16[2,512,128]{2,1,0:T(8,128)(2,1)S(1)}, u32[]{:S(2)}, u32[]{:S(2)}) collective-permute-start(bf16[2,512,128]{2,1,0:T(8,128)(2,1)S(1)} %pad_maximum_fusion), channel_id=1, source_target_pairs={{0,464},{16,480},{32,496},{48,0},{64,16},{80,32},{96,48},{112,64},... | collective-permute-start | bytes 786440 | tf_op jit(solution)/shard_map/ppermute | solution.py:17
  26.3 29.7 %collective-permute-start.1 = (bf16[2,512,128]{2,1,0:T(8,128)(2,1)S(1)}, bf16[2,512,128]{2,1,0:T(8,128)(2,1)S(1)}, u32[]{:S(2)}, u32[]{:S(2)}) collective-permute-start(bf16[2,512,128]{2,1,0:T(8,128)(2,1)S(1)} %pad_maximum_fusion), channel_id=1, source_target_pairs={{0,480},{16,496},{32,0},{48,16},{64,32},{80,48},{96,64},{112,80},{... | collective-permute-start | bytes 786440 | tf_op jit(solution)/shard_map/ppermute | solution.py:17
  33.0 27.3 %collective-permute-start = (bf16[2,512,128]{2,1,0:T(8,128)(2,1)S(1)}, bf16[2,512,128]{2,1,0:T(8,128)(2,1)S(1)}, u32[]{:S(2)}, u32[]{:S(2)}) collective-permute-start(bf16[2,512,128]{2,1,0:T(8,128)(2,1)S(1)} %pad_maximum_fusion), channel_id=1, source_target_pairs={{0,496},{16,0},{32,16},{48,32},{64,48},{80,64},{96,80},{112,96},{1... | collective-permute-start | bytes 786440 | tf_op jit(solution)/shard_map/ppermute | solution.py:17
  44.3 26.0 %copy-start.3 = (s32[6]{0:T(128)S(1)}, s32[6]{0:T(128)}, u32[]{:S(2)}) copy-start(s32[6]{0:T(128)} %constant.62.clone) | copy-start | bytes 76
  71.1 1.8 %copy-start.1 = (pred[512,7,512]{0,2,1:T(8,128)(4,1)S(1)}, pred[512,7,512]{0,2,1:T(8,128)(4,1)}, u32[]{:S(2)}) copy-start(pred[512,7,512]{0,2,1:T(8,128)(4,1)} %pad_add_fusion) | copy-start | bytes 5505028
  82.4 7.1 %copy-start.2 = (bf16[1,512,128]{1,2,0:T(8,128)(2,1)S(1)}, bf16[1,512,128]{1,2,0:T(8,128)(2,1)}, u32[]{:S(2)}) copy-start(bf16[1,512,128]{1,2,0:T(8,128)(2,1)} %copy.11) | copy-start | bytes 393220
Sparse Core Ops, SparseCore 0:
  97.1 48.2 all-gather.1
where the time goes:
time: 160 us; the launch traced here: 159 us
  waiting for transfers between devices  67.6 us (42%)
  starting transfers between devices  24.5 us (15%)
  matrix products  24.4 us (15%)
  local copies, waits for them, and re-layouts  18.3 us (11%)
  between operations  14.2 us (9%)
  other arithmetic  9.86 us (6%)
    all_gather x1, waiting for transfers between devices, on_device(): lax.all_gather(attended, 'mp', axis=1, tiled=True)  48.4 us
    ppermute x6, starting transfers between devices, shifted(): return lax.ppermute(value, axis, pairs)  24.5 us
    ppermute x6, waiting for transfers between devices, shifted(): return lax.ppermute(value, axis, pairs)  19.2 us
    another operation x7, local copies, waits for them, and re-layouts, on_device(): stacked = jnp.stack(neighbours)  12.9 us
    dot_general x1, matrix products, on_device(): jnp.einsum('ihd,sjd->hisj', query_rows, key_rows, preferred_element_type=...  9.58 us
    dot_general x1, matrix products, on_device(): jnp.einsum('hisj,sjd->ihd', weights, value_rows, preferred_element_type=j...  7.41 us
    reduce_sum x1, other arithmetic, on_device(): jnp.sum(expo, axis=(2, 3), keepdims=True)  7.14 us
    dot_general x1, matrix products, on_device(): jnp.dot(lax.all_gather(attended, 'mp', axis=1, tiled=True), out_weight, p...  6.61 us
  transfers between devices with their start and end apart: 7, of which 5 were waited for; matrix products, arithmetic and copies ran while one was open for 5% of the time, Pallas kernels for 0%

commit v1 on v0

--- a/solution.py
+++ b/solution.py
@@ -1,3 +1,4 @@
+import functools
 import math
 import jax
 import jax.numpy as jnp
@@ -9,6 +10,17 @@
 HD = 128
 REACH = 3
 SLOTS = 6
+
+
+def switch_pairs_all(inputs, dim_k):
+    local_out = jnp.concatenate(
+        lax.all_to_all(jnp.stack([inputs for _ in range(lax.axis_size("mp"))]), "mp", 0, 0),
+        axis=dim_k,
+    )
+    return local_out
+
+
+regions_state = functools.partial(switch_pairs_all, dim_k=1)
 
 
 def shifted(value, axis, steps):
@@ -62,11 +74,7 @@
     weights = (expo / jnp.sum(expo, axis=(2, 3), keepdims=True)).astype(jnp.bfloat16)
     attended = jnp.einsum("hisj,sjd->ihd", weights, value_rows, preferred_element_type=jnp.float32)
     attended = attended.astype(jnp.bfloat16).reshape(seq_len, heads_dev * HD)
-    judged = jnp.dot(
-        lax.all_gather(attended, "mp", axis=1, tiled=True),
-        out_weight,
-        preferred_element_type=jnp.float32,
-    )
+    judged = jnp.dot(regions_state(attended), out_weight, preferred_element_type=jnp.float32)
     return judged.astype(jnp.bfloat16)[None]
 
 

time: 160 us -> 203 us (1.27)
  blocking collectives: 0 us -> 109 us
  waiting for transfers between devices: 67.6 us -> 19.2 us
  between operations: 14.2 us -> 0.85 us
  matrix products: 24.4 us -> 20.2 us
    all_to_all x0 -> x1, blocking collectives: none -> 109 us  [switch_pairs_all(): lax.all_to_all(jnp.stack([inputs for _ in range(lax.axis_size('mp'))]), '...]
    all_gather x1 -> x0, waiting for transfers between devices: 48.4 us -> none  [on_device(): lax.all_gather(attended, 'mp', axis=1, tiled=True)]
    dot_general x1, matrix products: 6.61 us -> 3.15 us  [on_device(): jnp.dot(regions_state(attended), out_weight, preferred_element_type=jnp.f...]
  transfers between devices with their start and end apart: 7 -> 6, of which waited for: 5 -> 4; matrix products, arithmetic and copies ran while one was open for 5% -> 4% of each run, Pallas kernels for 0% -> 0%
where the time goes in v1:
time: 203 us; the launch traced here: 202 us
  blocking collectives  109 us (54%)
  starting transfers between devices  24.5 us (12%)
  matrix products  20.2 us (10%)
  waiting for transfers between devices  19.2 us (9%)
  local copies, waits for them, and re-layouts  18.7 us (9%)
  other arithmetic  9.87 us (5%)
    all_to_all x1, blocking collectives, switch_pairs_all(): lax.all_to_all(jnp.stack([inputs for _ in range(lax.axis_size('mp'))]), '...  109 us
    ppermute x6, starting transfers between devices, shifted(): return lax.ppermute(value, axis, pairs)  24.5 us
    ppermute x6, waiting for transfers between devices, shifted(): return lax.ppermute(value, axis, pairs)  19.2 us
    another operation x7, local copies, waits for them, and re-layouts, on_device(): stacked = jnp.stack(neighbours)  12.9 us
    dot_general x1, matrix products, on_device(): jnp.einsum('ihd,sjd->hisj', query_rows, key_rows, preferred_element_type=...  9.59 us
    reduce_sum x1, other arithmetic, on_device(): jnp.sum(expo, axis=(2, 3), keepdims=True)  7.14 us
    dot_general x1, matrix products, on_device(): jnp.einsum('hisj,sjd->ihd', weights, value_rows, preferred_element_type=j...  6.73 us
  transfers between devices with their start and end apart: 6, of which 4 were waited for; matrix products, arithmetic and copies ran while one was open for 4% of the time, Pallas kernels for 0%

profile of v1, /device:TPU:1, one launch (start us, length us, event | category | flops | bytes accessed | tf_op | source)
XLA Modules:
  0.0 202.0 jit_solution(3201608569179286030)
XLA Ops:
  0.0 0.0 copy-start
  0.0 0.0 copy-start.5
  0.0 1.0 constant_dynamic-slice_fusion.1
  1.1 6.1 %collective-permute-start.5 = (bf16[2,512,128]{2,1,0:T(8,128)(2,1)S(1)}, bf16[2,512,128]{2,1,0:T(8,128)(2,1)S(1)}, u32[]{:S(2)}, u32[]{:S(2)}) collective-permute-start(bf16[2,512,128]{2,1,0:T(8,128)(2,1)S(1)} %pad_maximum_fusion), channel_id=1, source_target_pairs={{0,48},{16,64},{32,80},{48,96},{64,112},{80,128},{96,144},{112,160... | collective-permute-start | bytes 786440 | tf_op jit(solution)/shard_map/ppermute | solution.py:29
  7.1 4.5 %collective-permute-start.4 = (bf16[2,512,128]{2,1,0:T(8,128)(2,1)S(1)}, bf16[2,512,128]{2,1,0:T(8,128)(2,1)S(1)}, u32[]{:S(2)}, u32[]{:S(2)}) collective-permute-start(bf16[2,512,128]{2,1,0:T(8,128)(2,1)S(1)} %pad_maximum_fusion), channel_id=1, source_target_pairs={{0,32},{16,48},{32,64},{48,80},{64,96},{80,112},{96,128},{112,144}... | collective-permute-start | bytes 786440 | tf_op jit(solution)/shard_map/ppermute | solution.py:29
  11.7 2.3 %collective-permute-start.3 = (bf16[2,512,128]{2,1,0:T(8,128)(2,1)S(1)}, bf16[2,512,128]{2,1,0:T(8,128)(2,1)S(1)}, u32[]{:S(2)}, u32[]{:S(2)}) collective-permute-start(bf16[2,512,128]{2,1,0:T(8,128)(2,1)S(1)} %pad_maximum_fusion), channel_id=1, source_target_pairs={{0,16},{16,32},{32,48},{48,64},{64,80},{80,96},{96,112},{112,128},... | collective-permute-start | bytes 786440 | tf_op jit(solution)/shard_map/ppermute | solution.py:29
  14.0 5.8 %collective-permute-start.2 = (bf16[2,512,128]{2,1,0:T(8,128)(2,1)S(1)}, bf16[2,512,128]{2,1,0:T(8,128)(2,1)S(1)}, u32[]{:S(2)}, u32[]{:S(2)}) collective-permute-start(bf16[2,512,128]{2,1,0:T(8,128)(2,1)S(1)} %pad_maximum_fusion), channel_id=1, source_target_pairs={{0,464},{16,480},{32,496},{48,0},{64,16},{80,32},{96,48},{112,64},... | collective-permute-start | bytes 786440 | tf_op jit(solution)/shard_map/ppermute | solution.py:29
  19.7 3.2 %collective-permute-start.1 = (bf16[2,512,128]{2,1,0:T(8,128)(2,1)S(1)}, bf16[2,512,128]{2,1,0:T(8,128)(2,1)S(1)}, u32[]{:S(2)}, u32[]{:S(2)}) collective-permute-start(bf16[2,512,128]{2,1,0:T(8,128)(2,1)S(1)} %pad_maximum_fusion), channel_id=1, source_target_pairs={{0,480},{16,496},{32,0},{48,16},{64,32},{80,48},{96,64},{112,80},{... | collective-permute-start | bytes 786440 | tf_op jit(solution)/shard_map/ppermute | solution.py:29
  23.0 0.1 iota_compare_fusion
  23.7 0.0 copy-done
  23.8 0.1 constant_dynamic-slice_fusion
  23.8 0.1 pad.4.clone
  23.9 1.9 pad_add_fusion
  25.8 0.7 compare_bitcast_fusion
  26.4 0.1 broadcast_select_fusion
  26.5 0.0 collective-permute-done.5
  26.5 2.6 %collective-permute-start = (bf16[2,512,128]{2,1,0:T(8,128)(2,1)S(1)}, bf16[2,512,128]{2,1,0:T(8,128)(2,1)S(1)}, u32[]{:S(2)}, u32[]{:S(2)}) collective-permute-start(bf16[2,512,128]{2,1,0:T(8,128)(2,1)S(1)} %pad_maximum_fusion), channel_id=1, source_target_pairs={{0,496},{16,0},{32,16},{48,32},{64,48},{80,64},{96,80},{112,96},{1... | collective-permute-start | bytes 786440 | tf_op jit(solution)/shard_map/ppermute | solution.py:29
  29.2 0.8 copy.17
  29.9 1.7 reshape_squeeze.3
  31.6 0.0 copy-done.5
  31.6 0.1 stack.35
  31.7 5.9 %collective-permute-done.4 = bf16[2,512,128]{2,1,0:T(8,128)(2,1)S(1)} collective-permute-done((bf16[2,512,128]{2,1,0:T(8,128)(2,1)S(1)}, bf16[2,512,128]{2,1,0:T(8,128)(2,1)S(1)}, u32[]{:S(2)}, u32[]{:S(2)}) %collective-permute-start.4) | collective-permute-done | bytes 262176 | tf_op jit(solution)/shard_map/ppermute | solution.py:29
  37.7 0.1 stack.34
  37.8 0.0 copy-start.3
  37.8 7.6 %collective-permute-done.3 = bf16[2,512,128]{2,1,0:T(8,128)(2,1)S(1)} collective-permute-done((bf16[2,512,128]{2,1,0:T(8,128)(2,1)S(1)}, bf16[2,512,128]{2,1,0:T(8,128)(2,1)S(1)}, u32[]{:S(2)}, u32[]{:S(2)}) %collective-permute-start.3) | collective-permute-done | bytes 262176 | tf_op jit(solution)/shard_map/ppermute | solution.py:29
  45.4 0.9 stack.33
  46.3 0.0 collective-permute-done.2
  46.3 0.9 stack.32
  47.2 2.3 %collective-permute-done.1 = bf16[2,512,128]{2,1,0:T(8,128)(2,1)S(1)} collective-permute-done((bf16[2,512,128]{2,1,0:T(8,128)(2,1)S(1)}, bf16[2,512,128]{2,1,0:T(8,128)(2,1)S(1)}, u32[]{:S(2)}, u32[]{:S(2)}) %collective-permute-start.1) | collective-permute-done | bytes 262176 | tf_op jit(solution)/shard_map/ppermute | solution.py:29
  49.5 0.9 stack.31
  50.4 3.4 %collective-permute-done = bf16[2,512,128]{2,1,0:T(8,128)(2,1)S(1)} collective-permute-done((bf16[2,512,128]{2,1,0:T(8,128)(2,1)S(1)}, bf16[2,512,128]{2,1,0:T(8,128)(2,1)S(1)}, u32[]{:S(2)}, u32[]{:S(2)}) %collective-permute-start) | collective-permute-done | bytes 262176 | tf_op jit(solution)/shard_map/ppermute | solution.py:29
  53.8 0.9 stack.30
  54.7 9.1 %stack.36 = bf16[6,131072]{1,0:T(8,128)(2,1)S(1)} concatenate(bf16[1,131072]{1,0:T(2,128)(2,1)} %stack.30, bf16[1,131072]{1,0:T(2,128)(2,1)} %stack.31, bf16[1,131072]{1,0:T(2,128)(2,1)} %stack.32, bf16[1,131072]{1,0:T(2,128)(2,1)} %stack.33, bf16[1,131072]{1,0:T(2,128)(2,1)S(1)} %stack.34, bf16[1,131072]{1,0:T(2,128)(2,1)S(1)} %stack.35), dimensions={0} | concatenate | bytes 3145728 | tf_op jit(solution)/shard_map/stack | solution.py:50
  63.8 0.0 copy-done.3
  63.8 0.8 fusion.3
  64.5 0.0 copy-start.1
  64.6 0.2 copy.27
  64.8 1.0 fusion.23
  65.8 0.3 copy.25
  66.1 0.3 copy-done.1
  66.3 9.6 %fusion.24 = (f32[2,512]{1,0:T(2,128)S(1)}, f32[2,512,7,512]{1,3,0,2:T(8,128)}) fusion(f32[2,7]{0,1:T(8,128)S(1)} %pad_bitcast_fusion, bf16[512,2,128]{2,1,0:T(2,128)(2,1)} %reshape_squeeze.3, bf16[6,512,128]{2,1,0:T(8,128)(2,1)} %get-tuple-element.6, bf16[1,512,128]{2,1,0:T(8,128)(2,1)S(1)} %get-tuple-element.11, pred[512,7,512]{0,2,1:T(8,128)(4,1)S(1)} %copy-done.1), kind=kOutput, calls=%fused_computation.47 | convolution fusion | flops 956038144 | bytes 17698872 | tf_op jit(solution)/shard_map/ihd,sjd->hisj/dot_general | solution.py:61
  75.9 0.0 copy-start.2
  75.9 7.1 %fusion.1 = f32[2,512]{1,0:T(2,128)S(1)} fusion(f32[2,512,7,512]{1,3,0,2:T(8,128)} %get-tuple-element.10, f32[2,512]{1,0:T(2,128)S(1)} %get-tuple-element.9), kind=kLoop, calls=%fused_computation.5 | loop fusion | flops 7339008 | bytes 14688256 | tf_op jit(solution)/shard_map/reduce_sum | solution.py:74
  83.1 0.0 copy-done.2
  83.1 6.7 %fusion.6 = bf16[128,2,512]{2,0,1:T(8,128)(2,1)S(1)} fusion(f32[2,512,7,512]{1,3,0,2:T(8,128)} %get-tuple-element.10, f32[2,512]{1,0:T(2,128)S(1)} %fusion.1, f32[2,512]{1,0:T(2,128)S(1)} %get-tuple-element.9, bf16[6,512,128]{1,2,0:T(8,128)(2,1)S(1)} %bitcast.62, bf16[1,512,128]{1,2,0:T(8,128)(2,1)S(1)} %copy-done.2), kind=kOutput, calls=%fused_computation.12 | convolution fusion | flops 952500224 | bytes 15867904 | tf_op jit(solution)/shard_map/hisj,sjd->ihd/dot_general | solution.py:75
  89.8 0.4 stack.37
  90.2 0.0 copy-start.4
  90.2 108.6 %all_to_all.5 = bf16[16,512,256]{1,2,0:T(8,128)(2,1)S(1)} all-to-all(bf16[16,512,256]{1,2,0:T(8,128)(2,1)S(1)} %stack.37), channel_id=1, replica_groups=mesh['resp'=32,'mp'=16] {'mp'}, dimensions={0} | all-to-all | bytes 8388608 | tf_op jit(solution)/shard_map/all_to_all | solution.py:17
  198.9 0.0 copy-done.4
  198.9 3.1 %fusion.4 = bf16[1,512,512]{2,1,0:T(8,128)(2,1)} fusion(bf16[512,4096]{0,1:T(8,128)(2,1)S(1)} %bitcast.61, bf16[4096,512]{1,0:T(8,128)(2,1)S(1)} %copy-done.4), kind=kOutput, calls=%fused_computation.10 | convolution fusion | flops 2147745792 | bytes 8912896 | tf_op jit(solution)/shard_map/dot_general | solution.py:77
  (5 shorter events, 0.1 us)
Async XLA Ops:
  0.0 23.7 %copy-start = (f32[2,32]{1,0:T(2,128)S(1)}, f32[2,32]{1,0:T(2,128)}, u32[]{:S(2)}) copy-start(f32[2,32]{1,0:T(2,128)} %param.13) | copy-start | bytes 772
  0.0 31.6 %copy-start.5 = (s32[1,6]{1,0:T(1,128)S(1)}, s32[1,6]{1,0:T(1,128)}, u32[]{:S(2)}) copy-start(s32[1,6]{1,0:T(1,128)} %param.14) | copy-start | bytes 76
  1.1 25.5 %collective-permute-start.5 = (bf16[2,512,128]{2,1,0:T(8,128)(2,1)S(1)}, bf16[2,512,128]{2,1,0:T(8,128)(2,1)S(1)}, u32[]{:S(2)}, u32[]{:S(2)}) collective-permute-start(bf16[2,512,128]{2,1,0:T(8,128)(2,1)S(1)} %pad_maximum_fusion), channel_id=1, source_target_pairs={{0,48},{16,64},{32,80},{48,96},{64,112},{80,128},{96,144},{112,160... | collective-permute-start | bytes 786440 | tf_op jit(solution)/shard_map/ppermute | solution.py:29
  7.1 30.5 %collective-permute-start.4 = (bf16[2,512,128]{2,1,0:T(8,128)(2,1)S(1)}, bf16[2,512,128]{2,1,0:T(8,128)(2,1)S(1)}, u32[]{:S(2)}, u32[]{:S(2)}) collective-permute-start(bf16[2,512,128]{2,1,0:T(8,128)(2,1)S(1)} %pad_maximum_fusion), channel_id=1, source_target_pairs={{0,32},{16,48},{32,64},{48,80},{64,96},{80,112},{96,128},{112,144}... | collective-permute-start | bytes 786440 | tf_op jit(solution)/shard_map/ppermute | solution.py:29
  11.7 33.7 %collective-permute-start.3 = (bf16[2,512,128]{2,1,0:T(8,128)(2,1)S(1)}, bf16[2,512,128]{2,1,0:T(8,128)(2,1)S(1)}, u32[]{:S(2)}, u32[]{:S(2)}) collective-permute-start(bf16[2,512,128]{2,1,0:T(8,128)(2,1)S(1)} %pad_maximum_fusion), channel_id=1, source_target_pairs={{0,16},{16,32},{32,48},{48,64},{64,80},{80,96},{96,112},{112,128},... | collective-permute-start | bytes 786440 | tf_op jit(solution)/shard_map/ppermute | solution.py:29
  14.0 32.3 %collective-permute-start.2 = (bf16[2,512,128]{2,1,0:T(8,128)(2,1)S(1)}, bf16[2,512,128]{2,1,0:T(8,128)(2,1)S(1)}, u32[]{:S(2)}, u32[]{:S(2)}) collective-permute-start(bf16[2,512,128]{2,1,0:T(8,128)(2,1)S(1)} %pad_maximum_fusion), channel_id=1, source_target_pairs={{0,464},{16,480},{32,496},{48,0},{64,16},{80,32},{96,48},{112,64},... | collective-permute-start | bytes 786440 | tf_op jit(solution)/shard_map/ppermute | solution.py:29
  19.7 29.7 %collective-permute-start.1 = (bf16[2,512,128]{2,1,0:T(8,128)(2,1)S(1)}, bf16[2,512,128]{2,1,0:T(8,128)(2,1)S(1)}, u32[]{:S(2)}, u32[]{:S(2)}) collective-permute-start(bf16[2,512,128]{2,1,0:T(8,128)(2,1)S(1)} %pad_maximum_fusion), channel_id=1, source_target_pairs={{0,480},{16,496},{32,0},{48,16},{64,32},{80,48},{96,64},{112,80},{... | collective-permute-start | bytes 786440 | tf_op jit(solution)/shard_map/ppermute | solution.py:29
  26.5 27.3 %collective-permute-start = (bf16[2,512,128]{2,1,0:T(8,128)(2,1)S(1)}, bf16[2,512,128]{2,1,0:T(8,128)(2,1)S(1)}, u32[]{:S(2)}, u32[]{:S(2)}) collective-permute-start(bf16[2,512,128]{2,1,0:T(8,128)(2,1)S(1)} %pad_maximum_fusion), channel_id=1, source_target_pairs={{0,496},{16,0},{32,16},{48,32},{64,48},{80,64},{96,80},{112,96},{1... | collective-permute-start | bytes 786440 | tf_op jit(solution)/shard_map/ppermute | solution.py:29
  37.8 26.0 %copy-start.3 = (s32[6]{0:T(128)S(1)}, s32[6]{0:T(128)}, u32[]{:S(2)}) copy-start(s32[6]{0:T(128)} %constant.62.clone) | copy-start | bytes 76
  64.5 1.8 copy-start.1
  75.9 7.1 %copy-start.2 = (bf16[1,512,128]{1,2,0:T(8,128)(2,1)S(1)}, bf16[1,512,128]{1,2,0:T(8,128)(2,1)}, u32[]{:S(2)}) copy-start(bf16[1,512,128]{1,2,0:T(8,128)(2,1)} %copy.17) | copy-start | bytes 393220
  90.2 108.7 %copy-start.4 = (bf16[4096,512]{1,0:T(8,128)(2,1)S(1)}, bf16[4096,512]{1,0:T(8,128)(2,1)}, u32[]{:S(2)}) copy-start(bf16[4096,512]{1,0:T(8,128)(2,1)} %param.12) | copy-start | bytes 12582916
